TPU v7x, 1024 devices: a whole 4x4x32 slice. The times are simulated.
1024 devices in a mesh: wide: 32 (over y, x, core), narrow: 32 (over z).
Axes of the slice: x: 4, y: 4, z: 32, core: 2. Of those that a mesh axis runs over, the one named last changes fastest.
Arguments:
- volumes: bfloat16 [32, 1, 4, 128, 4096], P('narrow', None, None, 'wide'), may hold values from -6 to 6
- first_kernel: bfloat16 [27, 32, 4], replicated, may hold values from -0.625 to 0.625
- second_kernel: bfloat16 [27, 64, 32], replicated, may hold values from -0.21875 to 0.21875
- cotangent: bfloat16 [32, 1, 64, 65536], P('narrow', None, None, 'wide'), may hold values from -6 to 6
Outputs:
- activations: bfloat16 [32, 1, 64, 65536], P('narrow', None, None, 'wide')
- weight_grad: float32 [27, 64, 32], P(None, 'narrow')
All inputs are finite; a program needn't handle non-finite values.
Results may differ from a plain program's by a relative error of at most 0.023.
The roundings to bfloat16 on the way count: a program that leaves them out, or rounds other values in their place, can miss the bound.
Values may be sent and summed in bfloat16 or wider, within the bound.
A program may use at most 32 MiB of HBM per device.

v0:
```python
import math

import jax
import jax.numpy as jnp
from jax import lax
from jax.sharding import PartitionSpec as P

CIN = 4
YCELLS = 64
XCELLS = 64


neg_slope = 0.3


def passed_along(block, axis, distance):
    devices = range(lax.axis_size(axis))
    route = [(i - distance, i) for i in devices if i - distance in devices]
    return lax.ppermute(block, axis, route)


def with_halo(x, sides, width):
    for axis, dim in sides:
        size, length = (lax.axis_size(axis), x.shape[dim])
        up = [(i, (i + 1) % size) for i in range(size - 1)]
        down = [(j, i) for i, j in up]
        last = lax.slice_in_dim(x, length - width, length, axis=dim)
        first = lax.slice_in_dim(x, 0, width, axis=dim)
        before = lax.ppermute(last, axis, up)
        after = lax.ppermute(first, axis, down)
        x = jnp.concatenate([before, x, after], axis=dim)
    return x


def split_up(x, dim, size):
    before, after = (x.shape[:dim], x.shape[dim + 1 :])
    return jnp.moveaxis(x.reshape(*before, size, -1, *after), dim, 0)


def summed_on_arrival(x, axis, dim):
    parts = split_up(x, dim, lax.axis_size(axis))
    arrived = lax.all_to_all(parts, axis, split_axis=0, concat_axis=0, tiled=True)
    return arrived.astype(jnp.float32).sum(axis=0)


def sent_to_all(x, axis):
    copies = jnp.broadcast_to(x, (lax.axis_size(axis), *x.shape))
    return lax.all_to_all(copies, axis, split_axis=0, concat_axis=0, tiled=True)


def taken_together(x, axis):
    everything = sent_to_all(x, axis)
    return jnp.sum(everything, axis=0)


def leaky_relu(value):
    return jnp.where(value > 0, value, neg_slope * value)


def edge_masks():
    half_x = XCELLS // 2
    plane = YCELLS // 2 * half_x
    column = jnp.arange(plane, dtype=jnp.int32) % half_x
    left_ok = jnp.where(column > 0, 1.0, 0.0).astype(jnp.bfloat16)
    right_ok = jnp.where(column < half_x - 1, 1.0, 0.0).astype(jnp.bfloat16)
    return (left_ok, right_ok)


def conv_first(stacked, out_depth, first_kernel):
    batch = stacked.shape[0]
    depth_in = stacked.shape[2]
    half_y = YCELLS // 2
    half_x = XCELLS // 2
    plane = half_y * half_x
    margin = half_x + 1
    left_ok, right_ok = edge_masks()
    grid = stacked.reshape(batch, CIN, depth_in, half_y, 2, half_x, 2)
    parity = grid.transpose(0, 1, 2, 4, 6, 3, 5).reshape(batch, CIN, depth_in, 2, 2, plane)
    flat = jnp.pad(parity, ((0, 0), (0, 0), (0, 0), (0, 0), (0, 0), (margin, 0)))
    pieces = []
    for shift_z in range(3):
        chosen = flat[:, :, shift_z : shift_z + 2 * out_depth - 1 : 2]
        for shift_y in range(3):
            row_par = 0 if shift_y == 1 else 1
            row_off = -1 if shift_y == 0 else 0
            for shift_x in range(3):
                col_par = 0 if shift_x == 1 else 1
                col_off = -1 if shift_x == 0 else 0
                begin = margin + row_off * half_x + col_off
                part = chosen[:, :, :, row_par, col_par, begin : begin + plane]
                if col_off == -1:
                    part = part * left_ok
                pieces.append(part)
    taps = jnp.stack(pieces, axis=1).reshape(batch, 27, CIN, out_depth * plane)
    total = jnp.einsum("toc,btcp->bop", first_kernel, taps, preferred_element_type=jnp.float32)
    first_act = leaky_relu(total).astype(jnp.bfloat16)
    return first_act.reshape(batch, first_kernel.shape[1], out_depth, plane)


def depth_taps(flat, shift_z, depth_out):
    half_x = XCELLS // 2
    plane = YCELLS // 2 * half_x
    margin = half_x + 1
    left_ok, right_ok = edge_masks()
    chosen = flat[:, :, shift_z : shift_z + depth_out]
    pieces = []
    for shift_y in range(3):
        for shift_x in range(3):
            begin = margin + (shift_y - 1) * half_x + (shift_x - 1)
            part = chosen[:, :, :, begin : begin + plane]
            if shift_x == 0:
                part = part * left_ok
            if shift_x == 2:
                part = part * right_ok
            pieces.append(part)
    stacked = jnp.stack(pieces, axis=1)
    return stacked.reshape(stacked.shape[0], 9, stacked.shape[2], depth_out * plane)


def body(volumes, first_kernel, second_kernel, cotangent):
    local = volumes[0]
    batch = local.shape[0]
    planes = local.shape[2]
    depth_out = planes // 2
    lower_plane = passed_along(local[:, :, planes - 1 :], "wide", 1)
    stacked = jnp.concatenate([lower_plane, local], axis=2)
    first_act = conv_first(stacked, depth_out, first_kernel)
    rimmed = with_halo(first_act, (("wide", 2),), 1)
    margin = XCELLS // 2 + 1
    flat = jnp.pad(rimmed, ((0, 0), (0, 0), (0, 0), (margin, margin)))
    cells_out = depth_out * (YCELLS // 2) * (XCELLS // 2)
    pre = jnp.zeros((batch, second_kernel.shape[1], cells_out), jnp.float32)
    for shift_z in range(3):
        taps = depth_taps(flat, shift_z, depth_out)
        pre = pre + jnp.einsum(
            "toc,btcp->bop",
            second_kernel[9 * shift_z : 9 * shift_z + 9],
            taps,
            preferred_element_type=jnp.float32,
        )
    output = leaky_relu(pre).astype(jnp.bfloat16)
    back = (cotangent[0].astype(jnp.float32) * jnp.where(pre > 0, 1.0, neg_slope)).astype(
        jnp.bfloat16
    )
    terms = []
    for shift_z in range(3):
        taps = depth_taps(flat, shift_z, depth_out)
        terms.append(jnp.einsum("bop,btcp->toc", back, taps, preferred_element_type=jnp.float32))
    count = lax.axis_size("wide") * lax.axis_size("narrow") * batch * cells_out
    local_term = jnp.concatenate(terms, axis=0) * (1.0 / math.sqrt(count))
    partial_rows = summed_on_arrival(local_term.astype(jnp.bfloat16), "narrow", 1)
    weight_grad = taken_together(partial_rows, "wide")
    return (output.reshape(1, batch, output.shape[1], cells_out), weight_grad)


def solution(mesh):
    return jax.shard_map(
        body,
        mesh=mesh,
        in_specs=(P("narrow", None, None, "wide", None), P(), P(), P("narrow", None, None, "wide")),
        out_specs=(P("narrow", None, None, "wide"), P(None, "narrow", None)),
        check_vma=False,
    )
```

profile of v0, /device:TPU:1, one launch (start us, length us, event | category | flops | bytes accessed | tf_op | source)
XLA Modules:
  0.0 169.0 jit_solution(7368143084866461274)
XLA Ops:
  0.6 1.0 slice.314
  1.6 4.5 %collective-permute-start = (bf16[1,4,1,4096]{3,2,1,0:T(2,128)(2,1)S(1)}, bf16[1,4,1,4096]{3,2,1,0:T(2,128)(2,1)S(1)}, u32[]{:S(2)}, u32[]{:S(2)}) collective-permute-start(bf16[1,4,1,4096]{3,2,1,0:T(2,128)(2,1)S(1)} %slice.314), channel_id=1, source_target_pairs={{0,32},{32,64},{64,96},{96,128},{128,160},{160,192},{192,224},{224... | collective-permute-start | bytes 98312 | tf_op jit(solution)/shard_map/ppermute | solution.py:19
  6.2 4.1 %copy.117 = bf16[1,1,4,4,4096]{3,4,2,1,0:T(8,128)(2,1)} copy(bf16[1,1,4,4,4096]{4,3,2,1,0:T(4,128)(2,1)} %param.4) | data formatting | bytes 262144 | tf_op args[0]
  10.2 10.7 %copy.119 = bf16[1,4,4,32,2,32,2]{5,3,6,4,2,1,0:T(8,128)(2,1)S(1)} copy(bf16[1,4,4,32,2,32,2]{2,6,5,4,3,1,0:T(2,128)(2,1)} %bitcast.122) | data formatting | bytes 262144 | tf_op jit(solution)/shard_map/concatenate | solution.py:126
  20.9 0.5 copy.116
  21.5 1.4 copy.118
  23.0 0.6 reshape.488
  24.3 0.7 fusion.45
  25.3 1.3 stack.186
  27.2 1.9 %collective-permute-start.1 = (bf16[1,32,1,1024]{3,2,1,0:T(2,128)(2,1)S(1)}, bf16[1,32,1,1024]{3,2,1,0:T(2,128)(2,1)S(1)}, u32[]{:S(2)}, u32[]{:S(2)}) collective-permute-start(bf16[1,32,1,1024]{3,2,1,0:T(2,128)(2,1)S(1)} %get-tuple-element.33), channel_id=1, source_target_pairs={{0,32},{32,64},{64,96},{96,128},{128,160},{160,192},{192,224},{224... | collective-permute-start | bytes 196616 | tf_op jit(solution)/shard_map/ppermute | solution.py:29
  29.1 12.4 %collective-permute-start.2 = (bf16[1,32,1,1024]{3,2,1,0:T(2,128)(2,1)S(1)}, bf16[1,32,1,1024]{3,2,1,0:T(2,128)(2,1)S(1)}, u32[]{:S(2)}, u32[]{:S(2)}) collective-permute-start(bf16[1,32,1,1024]{3,2,1,0:T(2,128)(2,1)S(1)} %get-tuple-element.34), channel_id=1, source_target_pairs={{32,0},{64,32},{96,64},{128,96},{160,128},{192,160},{224,192},{256... | collective-permute-start | bytes 196616 | tf_op jit(solution)/shard_map/ppermute | solution.py:30
  41.5 0.8 collective-permute-done.2
  42.3 1.0 select_maximum_fusion
  43.3 2.5 %slice_multiply_fusion.13 = (bf16[1,32,2,1024]{3,2,1,0:T(2,128)(2,1)}, bf16[1,32,2,1024]{3,2,1,0:T(2,128)(2,1)}, bf16[1,32,2,1024]{3,2,1,0:T(2,128)(2,1)}, bf16[...) fusion(bf16[1,32,4,1090]{3,2,1,0:T(4,128)(2,1)S(1)} %select_max, ...), kind=kLoop, calls=%fused_computation.53 | loop fusion | flops 589824 | bytes 2361344 | tf_op jit(solution)/shard_map/mul | solution.py:112
  45.9 3.3 %slice_multiply_fusion.12 = (bf16[1,32,2,1024]{3,2,1,0:T(2,128)(2,1)S(1)}, bf16[1,32,2,1024]{3,2,1,0:T(2,128)(2,1)S(1)}, bf16[1,32,2,1024]{3,2,1,0:T(2,128)(2,1)...) fusion(bf16[1,32,4,1090]{3,2,1,0:T(4,128)(2,1)S(1)} %select_max, ...), kind=kLoop, calls=%fused_computation.52 | loop fusion | flops 589824 | bytes 3934208 | tf_op jit(solution)/shard_map/mul | solution.py:114
  49.3 0.7 stack.188
  50.0 0.7 stack.189
  50.7 1.7 stack.190
  52.4 2.1 %pad_maximum_fusion.1 = (bf16[1,32,2,1024]{3,2,1,0:T(2,128)(2,1)S(1)}, bf16[1,32,2,1024]{3,2,1,0:T(2,128)(2,1)}) fusion(bf16[1,32,2,1024]{3,2,1,0:T(2,128)(2,1)S(1)} %reshape.490, bf16[1,32,1,1024]{3,2,1,0:T(2,128)(2,1)S(1)} %collective-permute-done.1, bf16[1,32,1,1024]{3,2,1,0:T(2,128)(2,1)} %copy-done.11), kind=kLoop, calls=%fused_computation.55 | loop fusion | flops 524288 | bytes 524288 | tf_op jit(solution)/shard_map/concatenate | solution.py:31
  54.5 0.7 stack.191
  55.2 0.7 stack.192
  55.9 1.6 stack.193
  57.6 0.7 stack.194
  58.3 0.7 stack.195
  59.0 0.7 stack.197
  59.7 0.9 constant_dynamic-update-slice_fusion.16
  60.7 1.6 stack.198
  62.3 1.6 stack.199
  63.9 1.6 stack.200
  65.5 0.9 constant_dynamic-update-slice_fusion.15
  66.5 0.9 constant_dynamic-update-slice_fusion.14
  67.4 0.9 constant_dynamic-update-slice_fusion.13
  68.3 1.8 %stack.202 = bf16[1,1,32,2048]{3,2,1,0:T(8,128)(2,1)} reshape(bf16[1,32,2,1024]{3,2,1,0:T(2,128)(2,1)} %get-tuple-element.8) | data formatting | bytes 262144 | tf_op jit(solution)/shard_map/stack | solution.py:116
  70.1 1.6 stack.203
  71.7 0.7 stack.204
  72.4 0.7 stack.205
  73.1 1.0 stack.211
  74.1 1.6 stack.207
  75.8 0.9 constant_dynamic-update-slice_fusion.25
  76.7 0.7 stack.208
  77.4 0.7 stack.209
  78.1 1.7 stack.210
  79.9 1.6 stack.213
  81.7 1.6 constant_dynamic-update-slice_fusion.12
  83.2 1.6 constant_dynamic-update-slice_fusion.11
  84.8 1.6 constant_dynamic-update-slice_fusion.10
  86.4 0.7 constant_dynamic-update-slice_fusion.9
  87.1 1.7 %convolution_bitcast_fusion.1 = f32[2048,64]{0,1:T(8,128)S(1)} fusion(bf16[1,9,32,2048]{3,2,1,0:T(8,128)(2,1)} %constant_dynamic-update-slice_fusion.9, bf16[27,64,32]{1,2,0:T(8,128)(2,1)} %param.6), kind=kOutput, calls=%fused_computation.1 | convolution fusion | flops 75497472 | bytes 1777664 | tf_op jit(solution)/shard_map/toc,btcp->bop/dot_general | solution.py:135
  89.0 0.7 copy-done.19
  91.3 1.2 fusion.34
  92.5 0.5 fusion.12
  93.0 0.8 copy-done.2
  93.8 0.5 fusion.15
  94.3 0.5 fusion.18
  95.2 0.6 fusion.27
  96.5 49.8 %all_to_all.10 = bf16[32,2,864]{2,1,0:T(2,128)(2,1)S(1)} all-to-all(bf16[32,2,864]{2,1,0:T(2,128)(2,1)S(1)} %reshape.502), channel_id=1, replica_groups=mesh['wide'=32,'narrow'=32] {'narrow'}, dimensions={0} | all-to-all | bytes 221184 | tf_op jit(solution)/shard_map/all_to_all | solution.py:42
  146.3 0.4 reshape.503
  146.8 0.5 convert_reduce_fusion
  147.5 1.0 reshape.504
  148.4 17.3 %all_to_all.11 = f32[32,1,1728]{2,1,0:T(1,128)S(1)} all-to-all(f32[32,1,1728]{2,1,0:T(1,128)S(1)} %reshape.504), channel_id=1, replica_groups=mesh['wide'=32,'narrow'=32] {'wide'}, dimensions={0} | all-to-all | bytes 442368 | tf_op jit(solution)/shard_map/all_to_all | solution.py:48
  165.7 0.5 broadcast.271
  166.2 1.2 reduce
  167.4 0.6 reshape.505
  168.0 1.0 reduce_sum.19
  (80 shorter events, 5.0 us)
Async XLA Ops:
  0.6 26.0 %copy-start = (bf16[27,32,4]{1,2,0:T(4,128)(2,1)S(1)}, bf16[27,32,4]{1,2,0:T(4,128)(2,1)}, u32[]{:S(2)}) copy-start(bf16[27,32,4]{1,2,0:T(4,128)(2,1)} %param.5) | copy-start | bytes 20740
  1.6 19.3 %collective-permute-start = (bf16[1,4,1,4096]{3,2,1,0:T(2,128)(2,1)S(1)}, bf16[1,4,1,4096]{3,2,1,0:T(2,128)(2,1)S(1)}, u32[]{:S(2)}, u32[]{:S(2)}) collective-permute-start(bf16[1,4,1,4096]{3,2,1,0:T(2,128)(2,1)S(1)} %slice.314), channel_id=1, source_target_pairs={{0,32},{32,64},{64,96},{96,128},{128,160},{160,192},{192,224},{224... | collective-permute-start | bytes 98312 | tf_op jit(solution)/shard_map/ppermute | solution.py:19
  27.2 14.4 %collective-permute-start.1 = (bf16[1,32,1,1024]{3,2,1,0:T(2,128)(2,1)S(1)}, bf16[1,32,1,1024]{3,2,1,0:T(2,128)(2,1)S(1)}, u32[]{:S(2)}, u32[]{:S(2)}) collective-permute-start(bf16[1,32,1,1024]{3,2,1,0:T(2,128)(2,1)S(1)} %get-tuple-element.33), channel_id=1, source_target_pairs={{0,32},{32,64},{64,96},{96,128},{128,160},{160,192},{192,224},{224... | collective-permute-start | bytes 196616 | tf_op jit(solution)/shard_map/ppermute | solution.py:29
  29.1 13.2 %collective-permute-start.2 = (bf16[1,32,1,1024]{3,2,1,0:T(2,128)(2,1)S(1)}, bf16[1,32,1,1024]{3,2,1,0:T(2,128)(2,1)S(1)}, u32[]{:S(2)}, u32[]{:S(2)}) collective-permute-start(bf16[1,32,1,1024]{3,2,1,0:T(2,128)(2,1)S(1)} %get-tuple-element.34), channel_id=1, source_target_pairs={{32,0},{64,32},{96,64},{128,96},{160,128},{192,160},{224,192},{256... | collective-permute-start | bytes 196616 | tf_op jit(solution)/shard_map/ppermute | solution.py:30
  42.3 3.5 %copy-start.11 = (bf16[1,32,1,1024]{3,2,1,0:T(2,128)(2,1)}, bf16[1,32,1,1024]{3,2,1,0:T(2,128)(2,1)S(1)}, u32[]{:S(2)}) copy-start(bf16[1,32,1,1024]{3,2,1,0:T(2,128)(2,1)S(1)} %collective-permute-done.2) | copy-start | bytes 196612
  50.7 8.3 %copy-start.17 = (bf16[1,32,2,1024]{3,2,1,0:T(2,128)(2,1)S(1)}, bf16[1,32,2,1024]{3,2,1,0:T(2,128)(2,1)}, u32[]{:S(2)}) copy-start(bf16[1,32,2,1024]{3,2,1,0:T(2,128)(2,1)} %get-tuple-element.19) | copy-start | bytes 393220
  68.3 5.8 %copy-start.1 = (bf16[1,9,32,2048]{3,2,1,0:T(8,128)(2,1)}, bf16[1,9,32,2048]{3,2,1,0:T(8,128)(2,1)S(1)}, u32[]{:S(2)}) copy-start(bf16[1,9,32,2048]{3,2,1,0:T(8,128)(2,1)S(1)} %bitcast_dynamic-update-slice_fusion) | copy-start | bytes 3538948
  78.1 8.3 %copy-start.13 = (bf16[1,1,32,2048]{3,2,1,0:T(8,128)(2,1)S(1)}, bf16[1,1,32,2048]{3,2,1,0:T(8,128)(2,1)}, u32[]{:S(2)}) copy-start(bf16[1,1,32,2048]{3,2,1,0:T(8,128)(2,1)} %stack.205) | copy-start | bytes 393220
  84.8 4.0 %copy-start.15 = (bf16[1,1,32,2048]{3,2,1,0:T(8,128)(2,1)S(1)}, bf16[1,1,32,2048]{3,2,1,0:T(8,128)(2,1)}, u32[]{:S(2)}) copy-start(bf16[1,1,32,2048]{3,2,1,0:T(8,128)(2,1)} %stack.208) | copy-start | bytes 393220
  86.4 2.5 %copy-start.16 = (bf16[1,1,32,2048]{3,2,1,0:T(8,128)(2,1)S(1)}, bf16[1,1,32,2048]{3,2,1,0:T(8,128)(2,1)}, u32[]{:S(2)}) copy-start(bf16[1,1,32,2048]{3,2,1,0:T(8,128)(2,1)} %stack.209) | copy-start | bytes 393220
  87.1 1.8 %copy-start.14 = (bf16[1,1,32,2048]{3,2,1,0:T(8,128)(2,1)S(1)}, bf16[1,1,32,2048]{3,2,1,0:T(8,128)(2,1)}, u32[]{:S(2)}) copy-start(bf16[1,1,32,2048]{3,2,1,0:T(8,128)(2,1)} %stack.210) | copy-start | bytes 393220
  87.1 1.9 %copy-start.12 = (bf16[1,1,32,2048]{3,2,1,0:T(8,128)(2,1)S(1)}, bf16[1,1,32,2048]{3,2,1,0:T(8,128)(2,1)}, u32[]{:S(2)}) copy-start(bf16[1,1,32,2048]{3,2,1,0:T(8,128)(2,1)} %stack.213) | copy-start | bytes 393220
  88.8 0.9 copy-start.19
  89.0 1.2 copy-start.4
  89.0 1.3 copy-start.5
  89.8 0.9 copy-start.3
  89.8 1.0 copy-start.10
  89.8 1.1 copy-start.9
  89.8 1.1 copy-start.8
  90.2 1.0 copy-start.7
  90.2 1.0 copy-start.6
  90.2 1.1 copy-start.18
  92.5 1.3 copy-start.2
where the time goes:
time: 170 us; the launch traced here: 169 us
  blocking collectives  67.1 us (39%)
  local copies, waits for them, and re-layouts  63.4 us (37%)
  starting transfers between devices  18.8 us (11%)
  other arithmetic  12.7 us (7%)
  matrix products  4.99 us (3%)
    all_to_all x1, blocking collectives, summed_on_arrival(): lax.all_to_all(parts, axis, split_axis=0, concat_axis=0, tiled=True)  49.8 us
    another operation x29, local copies, waits for them, and re-layouts, depth_taps(): stacked = jnp.stack(pieces, axis=1)  26.4 us
    unnamed x71, local copies, waits for them, and re-layouts  18.4 us
    all_to_all x1, blocking collectives, sent_to_all(): return lax.all_to_all(copies, axis, split_axis=0, concat_axis=0, tiled=True)  17.3 us
    ppermute x1, starting transfers between devices, with_halo(): after = lax.ppermute(first, axis, down)  12.4 us
    concatenate x2, local copies, waits for them, and re-layouts, body(): stacked = jnp.concatenate([lower_plane, local], axis=2)  12.1 us
    ppermute x1, starting transfers between devices, passed_along(): return lax.ppermute(block, axis, route)  4.51 us
  transfers between devices with their start and end apart: 3, of which 1 were waited for; matrix products, arithmetic and copies ran while one was open for 9% of the time, Pallas kernels for 0%

commit v1 on v0

v1 whole, which is shorter than its diff:
```python
import functools
import math

import jax
import jax.numpy as jnp
import numpy as np
from jax import lax
from jax.experimental import pallas as pl
from jax.experimental.pallas import tpu as pltpu
from jax.sharding import PartitionSpec as P

CIN = 4
C1 = 32
C2 = 64
HALF = 32
PLANE = HALF * HALF
SLOPE = 0.3
TAPS = 27
WIDTH = 896
ROWS2 = 9 * C1
F32 = jnp.float32
BF16 = jnp.bfloat16
MESH = pl.DeviceIdType.MESH


def lane_order():
    order = np.zeros((512, 512), np.float32)
    for k in range(4):
        for py in range(2):
            for x in range(64):
                order[k * 128 + py * 64 + x, (py * 2 + x % 2) * 128 + k * 32 + x // 2] = 1.0
    return order


def row_order():
    order = np.zeros((64, 64), np.float32)
    for z in range(4):
        for q in range(4):
            for ch in range(CIN):
                order[z * 16 + q * 4 + ch, q * 16 + ch * 4 + z] = 1.0
    return order


def first_places():
    places = np.zeros((TAPS, CIN, 256), np.float32)
    for t in range(TAPS):
        a, b, c = t // 9, t // 3 % 3, t % 3
        shift = (2 if b == 0 else 0) + (1 if c == 0 else 0)
        q = (0 if b == 1 else 2) + (0 if c == 1 else 1)
        for i in range(CIN):
            places[t, i, a * 64 + shift * 16 + q * 4 + i] = 1.0
    return places


def rolled(x, shift):
    return pltpu.roll(x, shift % PLANE, axis=1)


def kernel(
    n, scale, vol_ref, k1_ref, k2_ref, cot_ref, lanes_ref, rows_ref, places_ref,
    act_ref, grad_ref,
    raw, planes, taps1, taps2, weights2, spread, send1, recv1, send2, recv2, send3, final,
    halo_send, halo_recv, sem_send1, sem_recv1, sem_send2, sem_recv2, sem_send3, sem_recv3, ready,
):
    w = lax.axis_index("wide")
    z = lax.axis_index("narrow")
    gap = lax.rem(z - w + n, n)
    steps = jnp.minimum(gap, n - gap)
    owner = gap == 0
    above = lax.rem(z + 1, n)
    below = lax.rem(z + n - 1, n)
    barrier = pltpu.get_barrier_semaphore()

    def greet(k, carry):
        pl.semaphore_signal(barrier, 1, device_id={"wide": lax.rem(w + k, n)}, device_id_type=MESH)
        return carry

    lax.fori_loop(1, n, greet, 0)
    pl.semaphore_signal(barrier, 1, device_id={"narrow": above}, device_id_type=MESH)
    pl.semaphore_signal(barrier, 1, device_id={"narrow": below}, device_id_type=MESH)

    def announce(up, down):
        @pl.when(up)
        def _():
            pl.semaphore_signal(ready, 1, device_id={"narrow": above}, device_id_type=MESH)

        @pl.when(down)
        def _():
            pl.semaphore_signal(ready, 1, device_id={"narrow": below}, device_id_type=MESH)

    def relay(least, most):
        @pl.when((steps >= least) & (steps <= most))
        def _():
            pl.semaphore_wait(ready, 1)
            announce(gap < n // 2, gap > n // 2 + 1)

    for ch in range(CIN):
        raw[4 * ch : 4 * ch + 4, :] = vol_ref[ch].astype(F32)
    blocks = [raw[:, 512 * j : 512 * j + 512].astype(BF16) for j in range(8)]
    spreadout = jnp.dot(jnp.concatenate(blocks, axis=0), lanes_ref[...], preferred_element_type=F32).astype(BF16)
    joined = jnp.concatenate(
        [
            jnp.concatenate([spreadout[16 * j : 16 * j + 16, 128 * q : 128 * q + 128] for j in range(8)], axis=1)
            for q in range(4)
        ],
        axis=0,
    )
    planes[48:112, :] = jnp.dot(rows_ref[...], joined, preferred_element_type=F32).astype(BF16)

    first = w == 0
    last = w == n - 1

    @pl.when(first)
    def _():
        planes[0:48, :] = jnp.zeros((48, PLANE), BF16)

    @pl.when(last)
    def _():
        planes[112:144, :] = jnp.zeros((32, PLANE), BF16)

    pl.semaphore_wait(barrier, n + 1)

    upward = pltpu.make_async_remote_copy(
        planes.at[64:112], planes.at[0:48], halo_send.at[0], halo_recv.at[0],
        device_id={"wide": lax.rem(w + 1, n)}, device_id_type=MESH,
    )
    downward = pltpu.make_async_remote_copy(
        planes.at[48:80], planes.at[112:144], halo_send.at[1], halo_recv.at[1],
        device_id={"wide": lax.rem(w + n - 1, n)}, device_id_type=MESH,
    )

    @pl.when(jnp.logical_not(last))
    def _():
        upward.start()

    @pl.when(jnp.logical_not(first))
    def _():
        downward.start()

    @pl.when(owner)
    def _():
        announce(n > 1, n > 2)

    weights1 = jnp.zeros((C1, 256), F32)
    for t in range(TAPS):
        weights1 = weights1 + jnp.dot(k1_ref[t], places_ref[t], preferred_element_type=F32)
    weights1 = weights1[:, :192].astype(BF16)
    for k in range(7):
        pieces = [k2_ref[4 * k + r] if 4 * k + r < TAPS else jnp.zeros((C2, C1), BF16) for r in range(4)]
        weights2[:, 128 * k : 128 * k + 128] = jnp.concatenate(pieces, axis=1)

    lane = lax.broadcasted_iota(jnp.int32, (16, PLANE), 1)
    left_ok = (lane % HALF) != 0
    lower_ok = lane >= HALF

    def spread_plane(zi):
        base = planes[16 * zi : 16 * zi + 16, :].astype(F32)
        at_x = jnp.where(left_ok, rolled(base, 1), 0.0)
        at_y = jnp.where(lower_ok, rolled(base, HALF), 0.0)
        both = jnp.where(lower_ok, rolled(at_x, HALF), 0.0)
        for s, part in enumerate((base, at_x, at_y, both)):
            taps1[64 * zi + 16 * s : 64 * zi + 16 * s + 16, :] = part.astype(BF16)

    for zi in range(3, 7):
        spread_plane(zi)
    taps2[4 * ROWS2 :, :] = jnp.zeros((32, PLANE), BF16)

    @pl.when(jnp.logical_not(last))
    def _():
        upward.wait_send()
        downward.wait_recv()

    @pl.when(jnp.logical_not(first))
    def _():
        downward.wait_send()
        upward.wait_recv()

    relay(1, 4)

    for zi in (0, 1, 2, 7, 8):
        spread_plane(zi)

    lane2 = lax.broadcasted_iota(jnp.int32, (C1, PLANE), 1)
    left2 = (lane2 % HALF) != 0
    right2 = (lane2 % HALF) != HALF - 1
    lower2 = lane2 >= HALF
    upper2 = lane2 < PLANE - HALF

    for zo in range(4):
        pre = jnp.dot(weights1, taps1[128 * zo : 128 * zo + 192, :], preferred_element_type=F32)
        act = jnp.where(pre > 0, pre, SLOPE * pre)
        if zo == 3:
            act = jnp.where(last, 0.0, act)
        act = act.astype(BF16).astype(F32)
        across = (jnp.where(left2, rolled(act, 1), 0.0), act, jnp.where(right2, rolled(act, -1), 0.0))
        for c in range(3):
            parts = (
                jnp.where(lower2, rolled(across[c], HALF), 0.0),
                across[c],
                jnp.where(upper2, rolled(across[c], -HALF), 0.0),
            )
            for b in range(3):
                row = ROWS2 * zo + C1 * (3 * b + c)
                taps2[row : row + C1, :] = parts[b].astype(BF16)
        relay(5 + 2 * zo, 6 + 2 * zo)

    total = None
    for half in range(2):
        patches = taps2[ROWS2 * half : ROWS2 * half + WIDTH, :]
        pre = jnp.dot(weights2[...], patches, preferred_element_type=F32)
        cells = slice(PLANE * half, PLANE * half + PLANE)
        act_ref[:, cells] = jnp.where(pre > 0, pre, SLOPE * pre).astype(BF16)
        back = (cot_ref[:, cells].astype(F32) * jnp.where(pre > 0, 1.0, SLOPE)).astype(BF16)
        term = lax.dot_general(back, patches, (((1,), (1,)), ((), ())), preferred_element_type=F32)
        total = term if total is None else total + term
        relay(13 + 2 * half, 14 + 2 * half)
    relay(17, n)

    total = total * scale
    for k in range(7):
        spread[pl.ds(k, C2, stride=8), :] = total[:, 128 * k : 128 * k + 128]
    spread[pl.ds(7, C2, stride=8), :] = jnp.zeros((C2, 128), F32)
    size = C2 // n * 8
    send1[...] = spread[...].astype(BF16).reshape(n, size, 128)
    recv1[w] = send1[w]

    def scatter(k, carry):
        to = lax.rem(w + k, n)
        pltpu.make_async_remote_copy(
            send1.at[to], recv1.at[w], sem_send1, sem_recv1, device_id={"wide": to}, device_id_type=MESH
        ).start()
        return carry

    lax.fori_loop(1, n, scatter, 0)
    pltpu.make_async_copy(send1.at[pl.ds(0, n - 1)], send1.at[pl.ds(0, n - 1)], sem_send1).wait()
    pltpu.make_async_copy(recv1.at[pl.ds(0, n - 1)], recv1.at[pl.ds(0, n - 1)], sem_recv1).wait()

    send2[...] = jnp.sum(recv1[...].astype(F32), axis=0)

    deliver = pltpu.make_async_remote_copy(
        send2, recv2.at[z], sem_send2, sem_recv2, device_id={"narrow": w}, device_id_type=MESH
    )

    @pl.when(jnp.logical_not(owner))
    def _():
        deliver.start()
        deliver.wait_send()
        pltpu.make_async_copy(final, final, sem_recv3).wait()

    @pl.when(owner)
    def _():
        recv2[z] = send2[...]
        pltpu.make_async_copy(recv2.at[pl.ds(0, n - 1)], recv2.at[pl.ds(0, n - 1)], sem_recv2).wait()
        whole = jnp.sum(recv2[...], axis=0)
        send3[...] = whole
        final[...] = whole

        def hand_out(k, carry):
            pltpu.make_async_remote_copy(
                send3, final, sem_send3, sem_recv3, device_id={"wide": lax.rem(w + k, n)}, device_id_type=MESH
            ).start()
            return carry

        lax.fori_loop(1, n, hand_out, 0)
        pltpu.make_async_copy(recv2.at[pl.ds(0, n - 1)], recv2.at[pl.ds(0, n - 1)], sem_send3).wait()

    rows = C2 // n
    for t in range(TAPS):
        for r in range(rows):
            at = 8 * r + t // 4
            grad_ref[t, r : r + 1, :] = final[at : at + 1, C1 * (t % 4) : C1 * (t % 4) + C1]


def body(volumes, first_kernel, second_kernel, cotangent):
    n = lax.axis_size("wide")
    cells = cotangent.shape[3]
    scale = 1.0 / math.sqrt(n * lax.axis_size("narrow") * cells)
    size = C2 // n * 8
    vmem = pl.BlockSpec(memory_space=pltpu.VMEM)
    dma = pltpu.SemaphoreType.DMA
    act, grad = pl.pallas_call(
        functools.partial(kernel, n, scale),
        out_shape=(
            jax.ShapeDtypeStruct((C2, cells), BF16),
            jax.ShapeDtypeStruct((TAPS, C2 // n, C1), F32),
        ),
        in_specs=[vmem] * 7,
        out_specs=(vmem, vmem),
        scratch_shapes=[
            pltpu.VMEM((16, 4096), F32),
            pltpu.VMEM((144, PLANE), BF16),
            pltpu.VMEM((576, PLANE), BF16),
            pltpu.VMEM((4 * ROWS2 + 32, PLANE), BF16),
            pltpu.VMEM((C2, WIDTH), BF16),
            pltpu.VMEM((C2 * 8, 128), F32),
            pltpu.VMEM((n, size, 128), BF16),
            pltpu.VMEM((n, size, 128), BF16),
            pltpu.VMEM((size, 128), F32),
            pltpu.VMEM((n, size, 128), F32),
            pltpu.VMEM((size, 128), F32),
            pltpu.VMEM((size, 128), F32),
            dma((2,)),
            dma((2,)),
            dma(()),
            dma(()),
            dma(()),
            dma(()),
            dma(()),
            dma(()),
            pltpu.SemaphoreType.REGULAR,
        ],
        compiler_params=pltpu.CompilerParams(collective_id=0, has_side_effects=True),
    )(
        volumes.reshape(CIN, 4, 4096),
        first_kernel,
        second_kernel,
        cotangent.reshape(C2, cells),
        jnp.asarray(lane_order(), BF16),
        jnp.asarray(row_order(), BF16),
        jnp.asarray(first_places(), BF16),
    )
    return act.reshape(1, 1, C2, cells), grad


def solution(mesh):
    return jax.shard_map(
        body,
        mesh=mesh,
        in_specs=(P("narrow", None, None, "wide", None), P(), P(), P("narrow", None, None, "wide")),
        out_specs=(P("narrow", None, None, "wide"), P(None, "narrow", None)),
        check_vma=False,
    )
```

time: 170 us -> 67.3 us (0.40)
  the two profiles are of different devices: /device:TPU:1 before, /device:TPU:29 now
where the time goes in v1:
time: 67.3 us; the launch traced here: 67.1 us
  Pallas kernels  61.5 us (91%)
  local copies, waits for them, and re-layouts  4.96 us (7%)
    pallas_call x1, Pallas kernels, body(): pl.pallas_call(functools.partial(kernel, n, scale), out_shape=(jax.ShapeD...  61.5 us
    unnamed x8, local copies, waits for them, and re-layouts  4.96 us

profile of v1, /device:TPU:29, one launch (start us, length us, event | category | flops | bytes accessed | tf_op | source)
XLA Modules:
  0.0 67.1 jit_solution(8589129099670129013)
XLA Ops:
  0.6 0.0 copy-start
  0.6 1.7 %copy.9.k1_ref = bf16[27,32,4]{2,1,0:T(8,128)(2,1)} copy(bf16[27,32,4]{1,2,0:T(4,128)(2,1)} %param.8) | data formatting | bytes 13824 | tf_op args[1]
  2.4 0.0 copy-done
  2.4 1.0 %copy.10.k2_ref = bf16[27,64,32]{2,1,0:T(8,128)(2,1)} copy(bf16[27,64,32]{1,2,0:T(8,128)(2,1)S(1)} %copy-done) | data formatting | bytes 221184 | tf_op args[2]
  3.3 61.5 %shard_map.86 = (bf16[64,2048]{1,0:T(8,128)(2,1)}, f32[27,2,32]{2,1,0:T(2,128)}) custom-call(bf16[4,4,4096]{2,1,0:T(4,128)(2,1)} %bitcast.5, bf16[27,32,4]{2,1,0:T(8,128)(2,1)} %copy.9.k1_ref, bf16[27,64,32]{2,1,0:T(8,128)(2,1)} %copy.10.k2_ref, bf16[64,2048]{1,0:T(8,128)(2,1)} %bitcast.3, bf16[512,512]{1,0:T(8,128)(2,1)} %constant.6.clone.lanes_ref, ...), custom_call_target="tpu_custom_call" | custom-call | tf_op jit(solution)/shard_map/pallas_call | solution.py:281
  64.8 0.0 copy-start.1
  64.8 1.7 %copy.13 = bf16[1,1,64,2048]{3,2,1,0:T(8,128)(2,1)} copy(bf16[1,1,64,2048]{3,2,1,0:T(8,128)(2,1)} %bitcast.4) | data formatting | bytes 524288
  66.5 0.0 copy-done.1
  66.5 0.6 copy.14
Async XLA Ops:
  0.6 1.7 %copy-start = (bf16[27,64,32]{1,2,0:T(8,128)(2,1)S(1)}, bf16[27,64,32]{1,2,0:T(8,128)(2,1)}, u32[]{:S(2)}) copy-start(bf16[27,64,32]{1,2,0:T(8,128)(2,1)} %param.9) | copy-start | bytes 331780
  64.8 1.7 %copy-start.1 = (f32[27,2,32]{2,1,0:T(2,128)S(1)}, f32[27,2,32]{2,1,0:T(2,128)}, u32[]{:S(2)}) copy-start(f32[27,2,32]{2,1,0:T(2,128)} %get-tuple-element.9) | copy-start | bytes 20740

commit v2 on v1

--- a/solution.py
+++ b/solution.py
@@ -42,13 +42,13 @@
 
 
 def first_places():
-    places = np.zeros((TAPS, CIN, 256), np.float32)
+    places = np.zeros((256, 128), np.float32)
     for t in range(TAPS):
         a, b, c = t // 9, t // 3 % 3, t % 3
         shift = (2 if b == 0 else 0) + (1 if c == 0 else 0)
         q = (0 if b == 1 else 2) + (0 if c == 1 else 1)
         for i in range(CIN):
-            places[t, i, a * 64 + shift * 16 + q * 4 + i] = 1.0
+            places[a * 64 + shift * 16 + q * 4 + i, CIN * t + i] = 1.0
     return places
 
 
@@ -56,16 +56,23 @@
     return pltpu.roll(x, shift % PLANE, axis=1)
 
 
+def turned(x, size):
+    rows = lax.broadcasted_iota(jnp.int32, (size, size), 0)
+    columns = lax.broadcasted_iota(jnp.int32, (size, size), 1)
+    same = jnp.where(rows == columns, 1.0, 0.0).astype(BF16)
+    return lax.dot_general(same, x, (((1,), (1,)), ((), ())), preferred_element_type=F32).astype(BF16)
+
+
 def kernel(
-    n, scale, vol_ref, k1_ref, k2_ref, cot_ref, lanes_ref, rows_ref, places_ref,
+    n, scale, vol_hbm, lanes_hbm, rows_hbm, places_hbm, k1_hbm, k2_hbm, cot_hbm,
     act_ref, grad_ref,
-    raw, planes, taps1, taps2, weights2, spread, send1, recv1, send2, recv2, send3, final,
+    vol_ref, lanes_ref, rows_ref, places_ref, k1_ref, k2_ref, cot_ref, loads,
+    raw, stacked, planes, taps1, taps2, weights2, spread, send1, recv1, send2, recv2, send3, final,
     halo_send, halo_recv, sem_send1, sem_recv1, sem_send2, sem_recv2, sem_send3, sem_recv3, ready,
 ):
     w = lax.axis_index("wide")
     z = lax.axis_index("narrow")
     gap = lax.rem(z - w + n, n)
-    steps = jnp.minimum(gap, n - gap)
     owner = gap == 0
     above = lax.rem(z + 1, n)
     below = lax.rem(z + n - 1, n)
@@ -88,12 +95,22 @@
         def _():
             pl.semaphore_signal(ready, 1, device_id={"narrow": below}, device_id_type=MESH)
 
-    def relay(least, most):
-        @pl.when((steps >= least) & (steps <= most))
+    def relay():
+        @pl.when(jnp.logical_not(owner))
         def _():
             pl.semaphore_wait(ready, 1)
             announce(gap < n // 2, gap > n // 2 + 1)
 
+    pairs = (
+        (vol_hbm, vol_ref), (lanes_hbm, lanes_ref), (rows_hbm, rows_ref), (places_hbm, places_ref),
+        (k1_hbm, k1_ref), (k2_hbm, k2_ref), (cot_hbm, cot_ref),
+    )
+    copies = [pltpu.make_async_copy(source, target, loads.at[i]) for i, (source, target) in enumerate(pairs)]
+    for copy in copies:
+        copy.start()
+
+    for copy in copies[:3]:
+        copy.wait()
     for ch in range(CIN):
         raw[4 * ch : 4 * ch + 4, :] = vol_ref[ch].astype(F32)
     blocks = [raw[:, 512 * j : 512 * j + 512].astype(BF16) for j in range(8)]
@@ -141,13 +158,15 @@
     def _():
         announce(n > 1, n > 2)
 
-    weights1 = jnp.zeros((C1, 256), F32)
+    for copy in copies[3:]:
+        copy.wait()
     for t in range(TAPS):
-        weights1 = weights1 + jnp.dot(k1_ref[t], places_ref[t], preferred_element_type=F32)
-    weights1 = weights1[:, :192].astype(BF16)
-    for k in range(7):
-        pieces = [k2_ref[4 * k + r] if 4 * k + r < TAPS else jnp.zeros((C2, C1), BF16) for r in range(4)]
-        weights2[:, 128 * k : 128 * k + 128] = jnp.concatenate(pieces, axis=1)
+        stacked[CIN * t : CIN * t + CIN, :] = k1_ref[t].astype(F32)
+    stacked[CIN * TAPS :, :] = jnp.zeros((128 - CIN * TAPS, C1), F32)
+    placed = jnp.dot(places_ref[...], stacked[...].astype(BF16), preferred_element_type=F32).astype(BF16)
+    weights1 = turned(placed, C1)[:, :192]
+    weights2[:, : TAPS * C1] = turned(k2_ref[...].reshape(TAPS * C1, C2), C2)
+    weights2[:, TAPS * C1 :] = jnp.zeros((C2, WIDTH - TAPS * C1), BF16)
 
     lane = lax.broadcasted_iota(jnp.int32, (16, PLANE), 1)
     left_ok = (lane % HALF) != 0
@@ -174,8 +193,6 @@
     def _():
         downward.wait_send()
         upward.wait_recv()
-
-    relay(1, 4)
 
     for zi in (0, 1, 2, 7, 8):
         spread_plane(zi)
@@ -202,7 +219,6 @@
             for b in range(3):
                 row = ROWS2 * zo + C1 * (3 * b + c)
                 taps2[row : row + C1, :] = parts[b].astype(BF16)
-        relay(5 + 2 * zo, 6 + 2 * zo)
 
     total = None
     for half in range(2):
@@ -213,8 +229,6 @@
         back = (cot_ref[:, cells].astype(F32) * jnp.where(pre > 0, 1.0, SLOPE)).astype(BF16)
         term = lax.dot_general(back, patches, (((1,), (1,)), ((), ())), preferred_element_type=F32)
         total = term if total is None else total + term
-        relay(13 + 2 * half, 14 + 2 * half)
-    relay(17, n)
 
     total = total * scale
     for k in range(7):
@@ -232,6 +246,7 @@
         return carry
 
     lax.fori_loop(1, n, scatter, 0)
+    relay()
     pltpu.make_async_copy(send1.at[pl.ds(0, n - 1)], send1.at[pl.ds(0, n - 1)], sem_send1).wait()
     pltpu.make_async_copy(recv1.at[pl.ds(0, n - 1)], recv1.at[pl.ds(0, n - 1)], sem_recv1).wait()
 
@@ -278,16 +293,28 @@
     size = C2 // n * 8
     vmem = pl.BlockSpec(memory_space=pltpu.VMEM)
     dma = pltpu.SemaphoreType.DMA
+    inputs = (
+        volumes.reshape(CIN, 4, 4096),
+        jnp.asarray(lane_order(), BF16),
+        jnp.asarray(row_order(), BF16),
+        jnp.asarray(first_places(), BF16),
+        first_kernel.transpose(0, 2, 1),
+        second_kernel.transpose(0, 2, 1),
+        cotangent.reshape(C2, cells),
+    )
     act, grad = pl.pallas_call(
         functools.partial(kernel, n, scale),
         out_shape=(
             jax.ShapeDtypeStruct((C2, cells), BF16),
             jax.ShapeDtypeStruct((TAPS, C2 // n, C1), F32),
         ),
-        in_specs=[vmem] * 7,
+        in_specs=[pl.BlockSpec(memory_space=pltpu.HBM)] * 7,
         out_specs=(vmem, vmem),
         scratch_shapes=[
+            *[pltpu.VMEM(x.shape, BF16) for x in inputs],
+            dma((len(inputs),)),
             pltpu.VMEM((16, 4096), F32),
+            pltpu.VMEM((128, C1), F32),
             pltpu.VMEM((144, PLANE), BF16),
             pltpu.VMEM((576, PLANE), BF16),
             pltpu.VMEM((4 * ROWS2 + 32, PLANE), BF16),
@@ -309,16 +336,8 @@
             dma(()),
             pltpu.SemaphoreType.REGULAR,
         ],
-        compiler_params=pltpu.CompilerParams(collective_id=0, has_side_effects=True),
-    )(
-        volumes.reshape(CIN, 4, 4096),
-        first_kernel,
-        second_kernel,
-        cotangent.reshape(C2, cells),
-        jnp.asarray(lane_order(), BF16),
-        jnp.asarray(row_order(), BF16),
-        jnp.asarray(first_places(), BF16),
-    )
+        compiler_params=pltpu.CompilerParams(collective_id=0, has_side_effects=True, vmem_limit_bytes=24 << 20),
+    )(*[pltpu.with_memory_space_constraint(x, pltpu.HBM) for x in inputs])
     return act.reshape(1, 1, C2, cells), grad
 
 

time: 67.3 us -> 58.9 us (0.88)
  Pallas kernels: 61.5 us -> 56.8 us
  local copies, waits for them, and re-layouts: 4.96 us -> 1.31 us
    pallas_call x1, Pallas kernels: 61.5 us -> 56.8 us  [body(): pl.pallas_call(functools.partial(kernel, n, scale), out_shape=(jax.ShapeD...]
    unnamed x8 -> x2, local copies, waits for them, and re-layouts: 4.96 us -> 1.31 us
where the time goes in v2:
time: 58.9 us; the launch traced here: 58.7 us
  Pallas kernels  56.8 us (96%)
  local copies, waits for them, and re-layouts  1.31 us (2%)
  between operations  0.64 us (1%)
    pallas_call x1, Pallas kernels, body(): pl.pallas_call(functools.partial(kernel, n, scale), out_shape=(jax.ShapeD...  56.8 us
    unnamed x2, local copies, waits for them, and re-layouts  1.31 us

profile of v2, /device:TPU:29, one launch (start us, length us, event | category | flops | bytes accessed | tf_op | source)
XLA Modules:
  0.0 58.7 jit_solution(10507080611345106051)
XLA Ops:
  0.6 56.8 %shard_map.86 = (bf16[64,2048]{1,0:T(8,128)(2,1)S(1)}, f32[27,2,32]{2,1,0:T(2,128)S(1)}) custom-call(bf16[4,4,4096]{2,1,0:T(4,128)(2,1)} %bitcast.8, bf16[512,512]{1,0:T(8,128)(2,1)} %constant.6.clone.lanes_hbm, bf16[64,64]{1,0:T(8,128)(2,1)} %constant.7.clone.rows_hbm, bf16[256,128]{1,0:T(8,128)(2,1)} %constant.8.clone.places_hbm, ...), custom_call_target="tpu_custom_call" | custom-call | tf_op jit(solution)/shard_map/pallas_call | solution.py:305
  57.4 0.7 %copy.11 = bf16[1,1,64,2048]{3,2,1,0:T(8,128)(2,1)} copy(bf16[1,1,64,2048]{3,2,1,0:T(8,128)(2,1)S(1)} %bitcast.5) | data formatting | bytes 524288
  58.1 0.6 %copy.12 = f32[27,2,32]{2,1,0:T(2,128)} copy(f32[27,2,32]{2,1,0:T(2,128)S(1)} %get-tuple-element.9) | data formatting | bytes 13824

commit v3 on v2

--- a/solution.py
+++ b/solution.py
@@ -56,11 +56,11 @@
     return pltpu.roll(x, shift % PLANE, axis=1)
 
 
-def turned(x, size):
+def turned(x, size, kind=BF16):
     rows = lax.broadcasted_iota(jnp.int32, (size, size), 0)
     columns = lax.broadcasted_iota(jnp.int32, (size, size), 1)
     same = jnp.where(rows == columns, 1.0, 0.0).astype(BF16)
-    return lax.dot_general(same, x, (((1,), (1,)), ((), ())), preferred_element_type=F32).astype(BF16)
+    return lax.dot_general(same, x, (((1,), (1,)), ((), ())), preferred_element_type=F32).astype(kind)
 
 
 def kernel(
@@ -68,38 +68,104 @@
     act_ref, grad_ref,
     vol_ref, lanes_ref, rows_ref, places_ref, k1_ref, k2_ref, cot_ref, loads,
     raw, stacked, planes, taps1, taps2, weights2, spread, send1, recv1, send2, recv2, send3, final,
-    halo_send, halo_recv, sem_send1, sem_recv1, sem_send2, sem_recv2, sem_send3, sem_recv3, ready,
+    halo_send, halo_recv, sem_send1, sem_recv1, sem_send2, sem_recv2, sem_send3, sem_recv3,
+    ready_a, ready_b, meet_x, meet_y, meet_far, meet_core,
 ):
     w = lax.axis_index("wide")
     z = lax.axis_index("narrow")
-    gap = lax.rem(z - w + n, n)
-    owner = gap == 0
+    core = lax.rem(w, 2)
+    even, odd = core == 0, core == 1
+    owner = z == w
+    across = min(4, n // 2)
+    along = n // 2 // across
+    x = lax.rem(w // 2, across)
+    y = w // (2 * across)
+    partner = w + 1 - 2 * core
+    row_mates = [(y * across + lax.rem(x + k, across)) * 2 + core for k in sorted({1, across - 1} - {0})]
+    column_mates = [(lax.rem(y + k, along) * across + x) * 2 + core for k in sorted({1, along - 1} - {0}) if along > 1]
+    first = w == 0
+    last = w == n - 1
+    barrier = pltpu.get_barrier_semaphore()
+
+    def tell(semaphore, to):
+        pl.semaphore_signal(semaphore, 1, device_id=to, device_id_type=MESH)
+
+    @pl.when(jnp.logical_not(first))
+    def _():
+        tell(barrier, {"wide": w - 1})
+
+    @pl.when(jnp.logical_not(last))
+    def _():
+        tell(barrier, {"wide": w + 1})
+
+    for mate in row_mates + column_mates:
+        tell(barrier, {"wide": mate})
+
+    home_a = w - core
+    home_b = w - core + 1
+
+    def forwards(at, home):
+        gap = lax.rem(at - home + 2 * n, n)
+        reach = jnp.where(home > n // 2, n // 2, n - 1 - home)
+        return gap < reach, jnp.where(gap == 0, reach < n - 1, gap > reach + 1)
+
+    def sides(at):
+        up_a, down_a = forwards(at, home_a)
+        up_b, down_b = forwards(at, home_b)
+        return odd & (up_a | up_b), odd & (down_a | down_b)
+
     above = lax.rem(z + 1, n)
     below = lax.rem(z + n - 1, n)
-    barrier = pltpu.get_barrier_semaphore()
-
-    def greet(k, carry):
-        pl.semaphore_signal(barrier, 1, device_id={"wide": lax.rem(w + k, n)}, device_id_type=MESH)
-        return carry
-
-    lax.fori_loop(1, n, greet, 0)
-    pl.semaphore_signal(barrier, 1, device_id={"narrow": above}, device_id_type=MESH)
-    pl.semaphore_signal(barrier, 1, device_id={"narrow": below}, device_id_type=MESH)
-
-    def announce(up, down):
+
+    @pl.when(sides(below)[0])
+    def _():
+        tell(barrier, {"narrow": below})
+
+    @pl.when(sides(above)[1])
+    def _():
+        tell(barrier, {"narrow": above})
+
+    expects_above, expects_below = sides(z)
+
+    def meet(semaphore, mates):
+        for mate in mates:
+            tell(semaphore, {"wide": mate})
+
+    def met(semaphore, mates):
+        if mates:
+            pl.semaphore_wait(semaphore, len(mates))
+
+    def announce(semaphore, home):
+        up, down = forwards(z, home)
+
         @pl.when(up)
         def _():
-            pl.semaphore_signal(ready, 1, device_id={"narrow": above}, device_id_type=MESH)
+            tell(semaphore, {"narrow": above})
 
         @pl.when(down)
         def _():
-            pl.semaphore_signal(ready, 1, device_id={"narrow": below}, device_id_type=MESH)
+            tell(semaphore, {"narrow": below})
+
+    def pass_on(semaphore, home):
+        @pl.when(z != home)
+        def _():
+            pl.semaphore_wait(semaphore, 1)
+            announce(semaphore, home)
 
     def relay():
-        @pl.when(jnp.logical_not(owner))
+        @pl.when(odd)
         def _():
-            pl.semaphore_wait(ready, 1)
-            announce(gap < n // 2, gap > n // 2 + 1)
+            pass_on(ready_a, home_a)
+
+            @pl.when(z != home_a)
+            def _():
+                tell(ready_a, {"wide": partner})
+
+            pass_on(ready_b, home_b)
+
+        @pl.when(even & jnp.logical_not(owner))
+        def _():
+            pl.semaphore_wait(ready_a, 1)
 
     pairs = (
         (vol_hbm, vol_ref), (lanes_hbm, lanes_ref), (rows_hbm, rows_ref), (places_hbm, places_ref),
@@ -108,6 +174,20 @@
     copies = [pltpu.make_async_copy(source, target, loads.at[i]) for i, (source, target) in enumerate(pairs)]
     for copy in copies:
         copy.start()
+
+    greeted = len(row_mates) + len(column_mates)
+    for expected in (w > 0, w < n - 1, expects_above, expects_below):
+        greeted = greeted + jnp.where(expected, 1, 0)
+    pl.semaphore_wait(barrier, greeted)
+    meet(meet_x, row_mates)
+
+    @pl.when(odd & (z == home_a))
+    def _():
+        announce(ready_a, home_a)
+
+    @pl.when(odd & (z == home_b))
+    def _():
+        announce(ready_b, home_b)
 
     for copy in copies[:3]:
         copy.wait()
@@ -124,9 +204,6 @@
     )
     planes[48:112, :] = jnp.dot(rows_ref[...], joined, preferred_element_type=F32).astype(BF16)
 
-    first = w == 0
-    last = w == n - 1
-
     @pl.when(first)
     def _():
         planes[0:48, :] = jnp.zeros((48, PLANE), BF16)
@@ -134,8 +211,6 @@
     @pl.when(last)
     def _():
         planes[112:144, :] = jnp.zeros((32, PLANE), BF16)
-
-    pl.semaphore_wait(barrier, n + 1)
 
     upward = pltpu.make_async_remote_copy(
         planes.at[64:112], planes.at[0:48], halo_send.at[0], halo_recv.at[0],
@@ -154,9 +229,8 @@
     def _():
         downward.start()
 
-    @pl.when(owner)
-    def _():
-        announce(n > 1, n > 2)
+    met(meet_x, row_mates)
+    meet(meet_y, column_mates)
 
     for copy in copies[3:]:
         copy.wait()
@@ -183,19 +257,7 @@
     for zi in range(3, 7):
         spread_plane(zi)
     taps2[4 * ROWS2 :, :] = jnp.zeros((32, PLANE), BF16)
-
-    @pl.when(jnp.logical_not(last))
-    def _():
-        upward.wait_send()
-        downward.wait_recv()
-
-    @pl.when(jnp.logical_not(first))
-    def _():
-        downward.wait_send()
-        upward.wait_recv()
-
-    for zi in (0, 1, 2, 7, 8):
-        spread_plane(zi)
+    taps2[3 * ROWS2 : 3 * ROWS2 + 32, :] = jnp.zeros((32, PLANE), BF16)
 
     lane2 = lax.broadcasted_iota(jnp.int32, (C1, PLANE), 1)
     left2 = (lane2 % HALF) != 0
@@ -203,34 +265,57 @@
     lower2 = lane2 >= HALF
     upper2 = lane2 < PLANE - HALF
 
-    for zo in range(4):
+    def first_layer(zo):
         pre = jnp.dot(weights1, taps1[128 * zo : 128 * zo + 192, :], preferred_element_type=F32)
         act = jnp.where(pre > 0, pre, SLOPE * pre)
         if zo == 3:
             act = jnp.where(last, 0.0, act)
         act = act.astype(BF16).astype(F32)
-        across = (jnp.where(left2, rolled(act, 1), 0.0), act, jnp.where(right2, rolled(act, -1), 0.0))
+        shifted = (jnp.where(left2, rolled(act, 1), 0.0), act, jnp.where(right2, rolled(act, -1), 0.0))
         for c in range(3):
             parts = (
-                jnp.where(lower2, rolled(across[c], HALF), 0.0),
-                across[c],
-                jnp.where(upper2, rolled(across[c], -HALF), 0.0),
+                jnp.where(lower2, rolled(shifted[c], HALF), 0.0),
+                shifted[c],
+                jnp.where(upper2, rolled(shifted[c], -HALF), 0.0),
             )
             for b in range(3):
                 row = ROWS2 * zo + C1 * (3 * b + c)
                 taps2[row : row + C1, :] = parts[b].astype(BF16)
 
-    total = None
-    for half in range(2):
+    def second_layer(half):
         patches = taps2[ROWS2 * half : ROWS2 * half + WIDTH, :]
         pre = jnp.dot(weights2[...], patches, preferred_element_type=F32)
         cells = slice(PLANE * half, PLANE * half + PLANE)
         act_ref[:, cells] = jnp.where(pre > 0, pre, SLOPE * pre).astype(BF16)
         back = (cot_ref[:, cells].astype(F32) * jnp.where(pre > 0, 1.0, SLOPE)).astype(BF16)
-        term = lax.dot_general(back, patches, (((1,), (1,)), ((), ())), preferred_element_type=F32)
-        total = term if total is None else total + term
-
-    total = total * scale
+        return lax.dot_general(patches, back, (((1,), (1,)), ((), ())), preferred_element_type=F32)
+
+    first_layer(2)
+    met(meet_y, column_mates)
+    meet(meet_far, column_mates)
+
+    @pl.when(jnp.logical_not(last))
+    def _():
+        upward.wait_send()
+        downward.wait_recv()
+
+    @pl.when(jnp.logical_not(first))
+    def _():
+        downward.wait_send()
+        upward.wait_recv()
+
+    for zi in (0, 1, 2, 7, 8):
+        spread_plane(zi)
+    met(meet_far, column_mates)
+    tell(meet_core, {"wide": partner})
+    first_layer(0)
+    first_layer(1)
+    total = second_layer(0)
+    first_layer(3)
+    total = total + second_layer(1)
+    pl.semaphore_wait(meet_core, 1)
+
+    total = turned((total * scale).astype(BF16), C2, F32)
     for k in range(7):
         spread[pl.ds(k, C2, stride=8), :] = total[:, 128 * k : 128 * k + 128]
     spread[pl.ds(7, C2, stride=8), :] = jnp.zeros((C2, 128), F32)
@@ -250,7 +335,7 @@
     pltpu.make_async_copy(send1.at[pl.ds(0, n - 1)], send1.at[pl.ds(0, n - 1)], sem_send1).wait()
     pltpu.make_async_copy(recv1.at[pl.ds(0, n - 1)], recv1.at[pl.ds(0, n - 1)], sem_recv1).wait()
 
-    send2[...] = jnp.sum(recv1[...].astype(F32), axis=0)
+    send2[...] = jnp.sum(recv1[...].astype(F32), axis=0).astype(BF16)
 
     deliver = pltpu.make_async_remote_copy(
         send2, recv2.at[z], sem_send2, sem_recv2, device_id={"narrow": w}, device_id_type=MESH
@@ -266,7 +351,7 @@
     def _():
         recv2[z] = send2[...]
         pltpu.make_async_copy(recv2.at[pl.ds(0, n - 1)], recv2.at[pl.ds(0, n - 1)], sem_recv2).wait()
-        whole = jnp.sum(recv2[...], axis=0)
+        whole = jnp.sum(recv2[...].astype(F32), axis=0)
         send3[...] = whole
         final[...] = whole
 
@@ -277,7 +362,11 @@
             return carry
 
         lax.fori_loop(1, n, hand_out, 0)
-        pltpu.make_async_copy(recv2.at[pl.ds(0, n - 1)], recv2.at[pl.ds(0, n - 1)], sem_send3).wait()
+        def handed_out(k, carry):
+            pltpu.make_async_copy(send3, send3, sem_send3).wait()
+            return carry
+
+        lax.fori_loop(1, n, handed_out, 0)
 
     rows = C2 // n
     for t in range(TAPS):
@@ -322,8 +411,8 @@
             pltpu.VMEM((C2 * 8, 128), F32),
             pltpu.VMEM((n, size, 128), BF16),
             pltpu.VMEM((n, size, 128), BF16),
-            pltpu.VMEM((size, 128), F32),
-            pltpu.VMEM((n, size, 128), F32),
+            pltpu.VMEM((size, 128), BF16),
+            pltpu.VMEM((n, size, 128), BF16),
             pltpu.VMEM((size, 128), F32),
             pltpu.VMEM((size, 128), F32),
             dma((2,)),
@@ -334,7 +423,7 @@
             dma(()),
             dma(()),
             dma(()),
-            pltpu.SemaphoreType.REGULAR,
+            *[pltpu.SemaphoreType.REGULAR] * 6,
         ],
         compiler_params=pltpu.CompilerParams(collective_id=0, has_side_effects=True, vmem_limit_bytes=24 << 20),
     )(*[pltpu.with_memory_space_constraint(x, pltpu.HBM) for x in inputs])

time: 58.9 us -> 51.4 us (0.87)
  Pallas kernels: 56.8 us -> 49.3 us
    pallas_call x1, Pallas kernels: 56.8 us -> 49.3 us  [body(): pl.pallas_call(functools.partial(kernel, n, scale), out_shape=(jax.ShapeD...]
where the time goes in v3:
time: 51.4 us; the launch traced here: 51.2 us
  Pallas kernels  49.3 us (96%)
  local copies, waits for them, and re-layouts  1.31 us (3%)
  between operations  0.64 us (1%)
    pallas_call x1, Pallas kernels, body(): pl.pallas_call(functools.partial(kernel, n, scale), out_shape=(jax.ShapeD...  49.3 us
    unnamed x2, local copies, waits for them, and re-layouts  1.31 us

profile of v3, /device:TPU:29, one launch (start us, length us, event | category | flops | bytes accessed | tf_op | source)
XLA Modules:
  0.0 51.2 jit_solution(11577256503586359293)
XLA Ops:
  0.6 49.3 %shard_map.86 = (bf16[64,2048]{1,0:T(8,128)(2,1)S(1)}, f32[27,2,32]{2,1,0:T(2,128)S(1)}) custom-call(bf16[4,4,4096]{2,1,0:T(4,128)(2,1)} %bitcast.8, bf16[512,512]{1,0:T(8,128)(2,1)} %constant.6.clone.lanes_hbm, bf16[64,64]{1,0:T(8,128)(2,1)} %constant.7.clone.rows_hbm, bf16[256,128]{1,0:T(8,128)(2,1)} %constant.8.clone.places_hbm, ...), custom_call_target="tpu_custom_call" | custom-call | tf_op jit(solution)/shard_map/pallas_call | solution.py:394
  49.9 0.7 %copy.11 = bf16[1,1,64,2048]{3,2,1,0:T(8,128)(2,1)} copy(bf16[1,1,64,2048]{3,2,1,0:T(8,128)(2,1)S(1)} %bitcast.5) | data formatting | bytes 524288
  50.6 0.6 %copy.12 = f32[27,2,32]{2,1,0:T(2,128)} copy(f32[27,2,32]{2,1,0:T(2,128)S(1)} %get-tuple-element.9) | data formatting | bytes 13824

commit v4 on v3

--- a/solution.py
+++ b/solution.py
@@ -16,20 +16,10 @@
 PLANE = HALF * HALF
 SLOPE = 0.3
 TAPS = 27
-WIDTH = 896
 ROWS2 = 9 * C1
 F32 = jnp.float32
 BF16 = jnp.bfloat16
 MESH = pl.DeviceIdType.MESH
-
-
-def lane_order():
-    order = np.zeros((512, 512), np.float32)
-    for k in range(4):
-        for py in range(2):
-            for x in range(64):
-                order[k * 128 + py * 64 + x, (py * 2 + x % 2) * 128 + k * 32 + x // 2] = 1.0
-    return order
 
 
 def row_order():
@@ -64,12 +54,12 @@
 
 
 def kernel(
-    n, scale, vol_hbm, lanes_hbm, rows_hbm, places_hbm, k1_hbm, k2_hbm, cot_hbm,
+    n, scale, vol_hbm, rows_hbm, places_hbm, k1_hbm, k2_hbm, cot_hbm,
     act_ref, grad_ref,
-    vol_ref, lanes_ref, rows_ref, places_ref, k1_ref, k2_ref, cot_ref, loads,
-    raw, stacked, planes, taps1, taps2, weights2, spread, send1, recv1, send2, recv2, send3, final,
+    vol_ref, rows_ref, places_ref, k1_ref, k2_ref, cot_ref, loads,
+    raw, stacked, planes, taps1, taps2, weights2, parts2, backs, spread, send1, recv1, send2, recv2, send3, final,
     halo_send, halo_recv, sem_send1, sem_recv1, sem_send2, sem_recv2, sem_send3, sem_recv3,
-    ready_a, ready_b, meet_x, meet_y, meet_far, meet_core,
+    ready_a, ready_b, wrap_ok, meet_x, meet_y, meet_far, meet_core,
 ):
     w = lax.axis_index("wide")
     z = lax.axis_index("narrow")
@@ -104,15 +94,17 @@
     home_a = w - core
     home_b = w - core + 1
 
+    turn = min(n - 1, 26 * n // 32)
+
     def forwards(at, home):
         gap = lax.rem(at - home + 2 * n, n)
-        reach = jnp.where(home > n // 2, n // 2, n - 1 - home)
+        reach = jnp.where(home > n // 2, n // 2, turn - home)
         return gap < reach, jnp.where(gap == 0, reach < n - 1, gap > reach + 1)
 
     def sides(at):
         up_a, down_a = forwards(at, home_a)
         up_b, down_b = forwards(at, home_b)
-        return odd & (up_a | up_b), odd & (down_a | down_b)
+        return odd & (up_a | up_b), odd & (down_a | down_b) & (at != 0)
 
     above = lax.rem(z + 1, n)
     below = lax.rem(z + n - 1, n)
@@ -126,6 +118,15 @@
         tell(barrier, {"narrow": above})
 
     expects_above, expects_below = sides(z)
+
+    wrap_a, wrap_b = forwards(0, home_a)[1], forwards(0, home_b)[1]
+    wraps = odd & (wrap_a | wrap_b)
+
+    @pl.when(wraps & (z == 0))
+    def _():
+        tell(barrier, {"narrow": n - 1})
+
+    expects_first = wraps & (z == n - 1)
 
     def meet(semaphore, mates):
         for mate in mates:
@@ -142,7 +143,7 @@
         def _():
             tell(semaphore, {"narrow": above})
 
-        @pl.when(down)
+        @pl.when(down & (z > 0))
         def _():
             tell(semaphore, {"narrow": below})
 
@@ -161,14 +162,26 @@
             def _():
                 tell(ready_a, {"wide": partner})
 
+            @pl.when(wraps & (z == 0))
+            def _():
+                pl.semaphore_wait(wrap_ok, 1)
+
+            @pl.when(wrap_a & (z == 0))
+            def _():
+                tell(ready_a, {"narrow": n - 1})
+
             pass_on(ready_b, home_b)
+
+            @pl.when(wrap_b & (z == 0))
+            def _():
+                tell(ready_b, {"narrow": n - 1})
 
         @pl.when(even & jnp.logical_not(owner))
         def _():
             pl.semaphore_wait(ready_a, 1)
 
     pairs = (
-        (vol_hbm, vol_ref), (lanes_hbm, lanes_ref), (rows_hbm, rows_ref), (places_hbm, places_ref),
+        (vol_hbm, vol_ref), (rows_hbm, rows_ref), (places_hbm, places_ref),
         (k1_hbm, k1_ref), (k2_hbm, k2_ref), (cot_hbm, cot_ref),
     )
     copies = [pltpu.make_async_copy(source, target, loads.at[i]) for i, (source, target) in enumerate(pairs)]
@@ -176,11 +189,15 @@
         copy.start()
 
     greeted = len(row_mates) + len(column_mates)
-    for expected in (w > 0, w < n - 1, expects_above, expects_below):
+    for expected in (w > 0, w < n - 1, expects_above, expects_below, expects_first):
         greeted = greeted + jnp.where(expected, 1, 0)
     pl.semaphore_wait(barrier, greeted)
     meet(meet_x, row_mates)
 
+    @pl.when(expects_first)
+    def _():
+        tell(wrap_ok, {"narrow": 0})
+
     @pl.when(odd & (z == home_a))
     def _():
         announce(ready_a, home_a)
@@ -189,12 +206,16 @@
     def _():
         announce(ready_b, home_b)
 
-    for copy in copies[:3]:
+    source = lax.broadcasted_iota(jnp.int32, (512, 512), 0)
+    target = lax.broadcasted_iota(jnp.int32, (512, 512), 1)
+    goal = ((source // 64) % 2) * 256 + (source % 2) * 128 + (source // 128) * 32 + (source % 64) // 2
+    lanes = jnp.where(goal == target, 1.0, 0.0).astype(BF16)
+    for copy in copies[:2]:
         copy.wait()
     for ch in range(CIN):
         raw[4 * ch : 4 * ch + 4, :] = vol_ref[ch].astype(F32)
     blocks = [raw[:, 512 * j : 512 * j + 512].astype(BF16) for j in range(8)]
-    spreadout = jnp.dot(jnp.concatenate(blocks, axis=0), lanes_ref[...], preferred_element_type=F32).astype(BF16)
+    spreadout = jnp.dot(jnp.concatenate(blocks, axis=0), lanes, preferred_element_type=F32).astype(BF16)
     joined = jnp.concatenate(
         [
             jnp.concatenate([spreadout[16 * j : 16 * j + 16, 128 * q : 128 * q + 128] for j in range(8)], axis=1)
@@ -232,15 +253,15 @@
     met(meet_x, row_mates)
     meet(meet_y, column_mates)
 
-    for copy in copies[3:]:
+    for copy in copies[2:]:
         copy.wait()
     for t in range(TAPS):
         stacked[CIN * t : CIN * t + CIN, :] = k1_ref[t].astype(F32)
     stacked[CIN * TAPS :, :] = jnp.zeros((128 - CIN * TAPS, C1), F32)
     placed = jnp.dot(places_ref[...], stacked[...].astype(BF16), preferred_element_type=F32).astype(BF16)
     weights1 = turned(placed, C1)[:, :192]
-    weights2[:, : TAPS * C1] = turned(k2_ref[...].reshape(TAPS * C1, C2), C2)
-    weights2[:, TAPS * C1 :] = jnp.zeros((C2, WIDTH - TAPS * C1), BF16)
+    for a in range(3):
+        weights2[C2 * a : C2 * a + C2, :] = turned(k2_ref[9 * a : 9 * a + 9].reshape(ROWS2, C2), C2)
 
     lane = lax.broadcasted_iota(jnp.int32, (16, PLANE), 1)
     left_ok = (lane % HALF) != 0
@@ -256,8 +277,6 @@
 
     for zi in range(3, 7):
         spread_plane(zi)
-    taps2[4 * ROWS2 :, :] = jnp.zeros((32, PLANE), BF16)
-    taps2[3 * ROWS2 : 3 * ROWS2 + 32, :] = jnp.zeros((32, PLANE), BF16)
 
     lane2 = lax.broadcasted_iota(jnp.int32, (C1, PLANE), 1)
     left2 = (lane2 % HALF) != 0
@@ -282,15 +301,34 @@
                 row = ROWS2 * zo + C1 * (3 * b + c)
                 taps2[row : row + C1, :] = parts[b].astype(BF16)
 
-    def second_layer(half):
-        patches = taps2[ROWS2 * half : ROWS2 * half + WIDTH, :]
-        pre = jnp.dot(weights2[...], patches, preferred_element_type=F32)
+    reached = [[a for a in range(3) if 0 <= zo - a <= 1] for zo in range(4)]
+
+    def second_part(zo):
+        low, count = reached[zo][0], len(reached[zo])
+        parts2[zo, : C2 * count, :] = jnp.dot(
+            weights2[C2 * low : C2 * (low + count), :], taps2[ROWS2 * zo : ROWS2 * zo + ROWS2, :],
+            preferred_element_type=F32,
+        )
+
+    def second_sum(half):
+        pre = None
+        for a in range(3):
+            at = C2 * reached[half + a].index(a)
+            part = parts2[half + a, at : at + C2, :]
+            pre = part if pre is None else pre + part
         cells = slice(PLANE * half, PLANE * half + PLANE)
         act_ref[:, cells] = jnp.where(pre > 0, pre, SLOPE * pre).astype(BF16)
-        back = (cot_ref[:, cells].astype(F32) * jnp.where(pre > 0, 1.0, SLOPE)).astype(BF16)
-        return lax.dot_general(patches, back, (((1,), (1,)), ((), ())), preferred_element_type=F32)
+        backs[half] = (cot_ref[:, cells].astype(F32) * jnp.where(pre > 0, 1.0, SLOPE)).astype(BF16)
+
+    def gradient_part(zo):
+        columns = jnp.concatenate(
+            [backs[zo - a] if a in reached[zo] else jnp.zeros((C2, PLANE), BF16) for a in range(3)], axis=0
+        )
+        patches = taps2[ROWS2 * zo : ROWS2 * zo + ROWS2, :]
+        return lax.dot_general(patches, columns, (((1,), (1,)), ((), ())), preferred_element_type=F32)
 
     first_layer(2)
+    second_part(2)
     met(meet_y, column_mates)
     meet(meet_far, column_mates)
 
@@ -308,29 +346,39 @@
         spread_plane(zi)
     met(meet_far, column_mates)
     tell(meet_core, {"wide": partner})
-    first_layer(0)
-    first_layer(1)
-    total = second_layer(0)
+    for zo in (0, 1):
+        first_layer(zo)
+        second_part(zo)
+    second_sum(0)
     first_layer(3)
-    total = total + second_layer(1)
+    second_part(3)
+    second_sum(1)
+    total = gradient_part(0) + gradient_part(1) + gradient_part(2) + gradient_part(3)
+    total = (total * scale).astype(BF16)
+    total = jnp.concatenate([total[:, C2 * a : C2 * a + C2] for a in range(3)], axis=0)
+    total = turned(total, C2, F32)
     pl.semaphore_wait(meet_core, 1)
 
-    total = turned((total * scale).astype(BF16), C2, F32)
-    for k in range(7):
+    for k in range(6):
         spread[pl.ds(k, C2, stride=8), :] = total[:, 128 * k : 128 * k + 128]
+    rest = jnp.concatenate([total[:, 768:], jnp.zeros((C2, 896 - TAPS * C1), F32)], axis=1)
+    spread[pl.ds(6, C2, stride=8), :] = rest
     spread[pl.ds(7, C2, stride=8), :] = jnp.zeros((C2, 128), F32)
     size = C2 // n * 8
     send1[...] = spread[...].astype(BF16).reshape(n, size, 128)
     recv1[w] = send1[w]
 
-    def scatter(k, carry):
-        to = lax.rem(w + k, n)
+    far = [min(d, along - d) for d in range(along)], [min(d, across - d) for d in range(across)]
+    offsets = [(dy, dx, dc) for dy in range(along) for dx in range(across) for dc in range(2)][1:]
+    y_at = [lax.rem(y + d, along) * (2 * across) for d in range(along)]
+    x_at = [lax.rem(x + d, across) * 2 for d in range(across)]
+    core_at = [core, 1 - core]
+    order = sorted(offsets, key=lambda d: -(2 * far[0][d[0]] + 2 * far[1][d[1]] + d[2]))
+    mates = [y_at[dy] + x_at[dx] + core_at[dc] for dy, dx, dc in order]
+    for to in mates:
         pltpu.make_async_remote_copy(
             send1.at[to], recv1.at[w], sem_send1, sem_recv1, device_id={"wide": to}, device_id_type=MESH
         ).start()
-        return carry
-
-    lax.fori_loop(1, n, scatter, 0)
     relay()
     pltpu.make_async_copy(send1.at[pl.ds(0, n - 1)], send1.at[pl.ds(0, n - 1)], sem_send1).wait()
     pltpu.make_async_copy(recv1.at[pl.ds(0, n - 1)], recv1.at[pl.ds(0, n - 1)], sem_recv1).wait()
@@ -351,28 +399,23 @@
     def _():
         recv2[z] = send2[...]
         pltpu.make_async_copy(recv2.at[pl.ds(0, n - 1)], recv2.at[pl.ds(0, n - 1)], sem_recv2).wait()
-        whole = jnp.sum(recv2[...].astype(F32), axis=0)
+        whole = jnp.sum(recv2[...].astype(F32), axis=0).astype(BF16)
         send3[...] = whole
         final[...] = whole
 
-        def hand_out(k, carry):
+        for to in mates:
             pltpu.make_async_remote_copy(
-                send3, final, sem_send3, sem_recv3, device_id={"wide": lax.rem(w + k, n)}, device_id_type=MESH
+                send3, final, sem_send3, sem_recv3, device_id={"wide": to}, device_id_type=MESH
             ).start()
-            return carry
-
-        lax.fori_loop(1, n, hand_out, 0)
-        def handed_out(k, carry):
-            pltpu.make_async_copy(send3, send3, sem_send3).wait()
-            return carry
-
-        lax.fori_loop(1, n, handed_out, 0)
+
+        pltpu.make_async_copy(recv2.at[pl.ds(0, n - 1)], recv2.at[pl.ds(0, n - 1)], sem_send3).wait()
 
     rows = C2 // n
+    result = final[...].astype(F32)
     for t in range(TAPS):
         for r in range(rows):
             at = 8 * r + t // 4
-            grad_ref[t, r : r + 1, :] = final[at : at + 1, C1 * (t % 4) : C1 * (t % 4) + C1]
+            grad_ref[t, r : r + 1, :] = result[at : at + 1, C1 * (t % 4) : C1 * (t % 4) + C1]
 
 
 def body(volumes, first_kernel, second_kernel, cotangent):
@@ -384,7 +427,6 @@
     dma = pltpu.SemaphoreType.DMA
     inputs = (
         volumes.reshape(CIN, 4, 4096),
-        jnp.asarray(lane_order(), BF16),
         jnp.asarray(row_order(), BF16),
         jnp.asarray(first_places(), BF16),
         first_kernel.transpose(0, 2, 1),
@@ -397,7 +439,7 @@
             jax.ShapeDtypeStruct((C2, cells), BF16),
             jax.ShapeDtypeStruct((TAPS, C2 // n, C1), F32),
         ),
-        in_specs=[pl.BlockSpec(memory_space=pltpu.HBM)] * 7,
+        in_specs=[pl.BlockSpec(memory_space=pltpu.HBM)] * len(inputs),
         out_specs=(vmem, vmem),
         scratch_shapes=[
             *[pltpu.VMEM(x.shape, BF16) for x in inputs],
@@ -406,15 +448,17 @@
             pltpu.VMEM((128, C1), F32),
             pltpu.VMEM((144, PLANE), BF16),
             pltpu.VMEM((576, PLANE), BF16),
-            pltpu.VMEM((4 * ROWS2 + 32, PLANE), BF16),
-            pltpu.VMEM((C2, WIDTH), BF16),
+            pltpu.VMEM((4 * ROWS2, PLANE), BF16),
+            pltpu.VMEM((3 * C2, ROWS2), BF16),
+            pltpu.VMEM((4, 2 * C2, PLANE), F32),
+            pltpu.VMEM((2, C2, PLANE), BF16),
             pltpu.VMEM((C2 * 8, 128), F32),
             pltpu.VMEM((n, size, 128), BF16),
             pltpu.VMEM((n, size, 128), BF16),
             pltpu.VMEM((size, 128), BF16),
             pltpu.VMEM((n, size, 128), BF16),
-            pltpu.VMEM((size, 128), F32),
-            pltpu.VMEM((size, 128), F32),
+            pltpu.VMEM((size, 128), BF16),
+            pltpu.VMEM((size, 128), BF16),
             dma((2,)),
             dma((2,)),
             dma(()),
@@ -423,7 +467,7 @@
             dma(()),
             dma(()),
             dma(()),
-            *[pltpu.SemaphoreType.REGULAR] * 6,
+            *[pltpu.SemaphoreType.REGULAR] * 7,
         ],
         compiler_params=pltpu.CompilerParams(collective_id=0, has_side_effects=True, vmem_limit_bytes=24 << 20),
     )(*[pltpu.with_memory_space_constraint(x, pltpu.HBM) for x in inputs])

time: 51.4 us -> 51.3 us (level)
  the two profiles are of different devices: /device:TPU:29 before, /device:TPU:17 now
where the time goes in v4:
time: 51.3 us; the launch traced here: 51.1 us
  Pallas kernels  49.1 us (96%)
  local copies, waits for them, and re-layouts  1.31 us (3%)
  between operations  0.64 us (1%)
    pallas_call x1, Pallas kernels, body(): pl.pallas_call(functools.partial(kernel, n, scale), out_shape=(jax.ShapeD...  49.1 us
    unnamed x2, local copies, waits for them, and re-layouts  1.31 us

profile of v4, /device:TPU:17, one launch (start us, length us, event | category | flops | bytes accessed | tf_op | source)
XLA Modules:
  0.0 51.1 jit_solution(15064228419486862389)
XLA Ops:
  0.6 49.1 %shard_map.77 = (bf16[64,2048]{1,0:T(8,128)(2,1)S(1)}, f32[27,2,32]{2,1,0:T(2,128)S(1)}) custom-call(bf16[4,4,4096]{2,1,0:T(4,128)(2,1)} %bitcast.8, bf16[64,64]{1,0:T(8,128)(2,1)} %constant.4.clone.rows_hbm, bf16[256,128]{1,0:T(8,128)(2,1)} %constant.5.clone.places_hbm, bf16[27,4,32]{2,1,0:T(4,128)(2,1)} %bitcast.9, bf16[27,32,64]{2,1,0:T(8,128)(2,1)} %bitcast.7, ...), custom_call_target="tpu_custom_call" | custom-call | tf_op jit(solution)/shard_map/pallas_call | solution.py:436
  49.8 0.7 %copy.10 = bf16[1,1,64,2048]{3,2,1,0:T(8,128)(2,1)} copy(bf16[1,1,64,2048]{3,2,1,0:T(8,128)(2,1)S(1)} %bitcast.5) | data formatting | bytes 524288
  50.5 0.6 %copy.11 = f32[27,2,32]{2,1,0:T(2,128)} copy(f32[27,2,32]{2,1,0:T(2,128)S(1)} %get-tuple-element.9) | data formatting | bytes 13824

commit v5 on v4

--- a/solution.py
+++ b/solution.py
@@ -59,7 +59,7 @@
     vol_ref, rows_ref, places_ref, k1_ref, k2_ref, cot_ref, loads,
     raw, stacked, planes, taps1, taps2, weights2, parts2, backs, spread, send1, recv1, send2, recv2, send3, final,
     halo_send, halo_recv, sem_send1, sem_recv1, sem_send2, sem_recv2, sem_send3, sem_recv3,
-    ready_a, ready_b, wrap_ok, meet_x, meet_y, meet_far, meet_core,
+    ready_a, ready_b, wrap_ok, near1, near2, near3,
 ):
     w = lax.axis_index("wide")
     z = lax.axis_index("narrow")
@@ -88,17 +88,19 @@
     def _():
         tell(barrier, {"wide": w + 1})
 
-    for mate in row_mates + column_mates:
+    mates_near = row_mates + column_mates
+    for mate in mates_near:
         tell(barrier, {"wide": mate})
+        tell(barrier, {"wide": mate + 1 - 2 * core})
 
     home_a = w - core
     home_b = w - core + 1
 
-    turn = min(n - 1, 26 * n // 32)
+    turn = min(n - 1, 3 * n // 4 + 1)
 
     def forwards(at, home):
         gap = lax.rem(at - home + 2 * n, n)
-        reach = jnp.where(home > n // 2, n // 2, turn - home)
+        reach = jnp.where(home > n // 2, n // 2, jnp.where(home == n // 2, n - 1, turn) - home)
         return gap < reach, jnp.where(gap == 0, reach < n - 1, gap > reach + 1)
 
     def sides(at):
@@ -188,11 +190,11 @@
     for copy in copies:
         copy.start()
 
-    greeted = len(row_mates) + len(column_mates)
+    greeted = 2 * len(mates_near)
     for expected in (w > 0, w < n - 1, expects_above, expects_below, expects_first):
         greeted = greeted + jnp.where(expected, 1, 0)
     pl.semaphore_wait(barrier, greeted)
-    meet(meet_x, row_mates)
+    meet(near1, mates_near)
 
     @pl.when(expects_first)
     def _():
@@ -250,8 +252,8 @@
     def _():
         downward.start()
 
-    met(meet_x, row_mates)
-    meet(meet_y, column_mates)
+    met(near1, mates_near)
+    meet(near2, mates_near)
 
     for copy in copies[2:]:
         copy.wait()
@@ -329,8 +331,8 @@
 
     first_layer(2)
     second_part(2)
-    met(meet_y, column_mates)
-    meet(meet_far, column_mates)
+    met(near2, mates_near)
+    meet(near3, mates_near)
 
     @pl.when(jnp.logical_not(last))
     def _():
@@ -344,8 +346,6 @@
 
     for zi in (0, 1, 2, 7, 8):
         spread_plane(zi)
-    met(meet_far, column_mates)
-    tell(meet_core, {"wide": partner})
     for zo in (0, 1):
         first_layer(zo)
         second_part(zo)
@@ -357,7 +357,7 @@
     total = (total * scale).astype(BF16)
     total = jnp.concatenate([total[:, C2 * a : C2 * a + C2] for a in range(3)], axis=0)
     total = turned(total, C2, F32)
-    pl.semaphore_wait(meet_core, 1)
+    met(near3, mates_near)
 
     for k in range(6):
         spread[pl.ds(k, C2, stride=8), :] = total[:, 128 * k : 128 * k + 128]
@@ -467,7 +467,7 @@
             dma(()),
             dma(()),
             dma(()),
-            *[pltpu.SemaphoreType.REGULAR] * 7,
+            *[pltpu.SemaphoreType.REGULAR] * 6,
         ],
         compiler_params=pltpu.CompilerParams(collective_id=0, has_side_effects=True, vmem_limit_bytes=24 << 20),
     )(*[pltpu.with_memory_space_constraint(x, pltpu.HBM) for x in inputs])

time: 51.3 us -> 50.6 us (0.986)
  the two profiles are of different devices: /device:TPU:17 before, /device:TPU:1 now
where the time goes in v5:
time: 50.6 us; the launch traced here: 50 us
  Pallas kernels  48 us (95%)
  local copies, waits for them, and re-layouts  1.31 us (3%)
  between operations  0.64 us (1%)
    pallas_call x1, Pallas kernels, body(): pl.pallas_call(functools.partial(kernel, n, scale), out_shape=(jax.ShapeD...  48 us
    unnamed x2, local copies, waits for them, and re-layouts  1.31 us

profile of v5, /device:TPU:1, one launch (start us, length us, event | category | flops | bytes accessed | tf_op | source)
XLA Modules:
  0.0 50.0 jit_solution(13595832957547883774)
XLA Ops:
  0.6 48.0 %shard_map.77 = (bf16[64,2048]{1,0:T(8,128)(2,1)S(1)}, f32[27,2,32]{2,1,0:T(2,128)S(1)}) custom-call(bf16[4,4,4096]{2,1,0:T(4,128)(2,1)} %bitcast.8, bf16[64,64]{1,0:T(8,128)(2,1)} %constant.4.clone.rows_hbm, bf16[256,128]{1,0:T(8,128)(2,1)} %constant.5.clone.places_hbm, bf16[27,4,32]{2,1,0:T(4,128)(2,1)} %bitcast.9, bf16[27,32,64]{2,1,0:T(8,128)(2,1)} %bitcast.7, ...), custom_call_target="tpu_custom_call" | custom-call | tf_op jit(solution)/shard_map/pallas_call | solution.py:436
  48.7 0.7 %copy.10 = bf16[1,1,64,2048]{3,2,1,0:T(8,128)(2,1)} copy(bf16[1,1,64,2048]{3,2,1,0:T(8,128)(2,1)S(1)} %bitcast.5) | data formatting | bytes 524288
  49.4 0.6 %copy.11 = f32[27,2,32]{2,1,0:T(2,128)} copy(f32[27,2,32]{2,1,0:T(2,128)S(1)} %get-tuple-element.9) | data formatting | bytes 13824

commit v6 on v5

--- a/solution.py
+++ b/solution.py
@@ -65,7 +65,6 @@
     z = lax.axis_index("narrow")
     core = lax.rem(w, 2)
     even, odd = core == 0, core == 1
-    owner = z == w
     across = min(4, n // 2)
     along = n // 2 // across
     x = lax.rem(w // 2, across)
@@ -95,6 +94,8 @@
 
     home_a = w - core
     home_b = w - core + 1
+    own_a, own_b = odd & (z == home_a), odd & (z == home_b)
+    owner = own_a | own_b
 
     turn = min(n - 1, 3 * n // 4 + 1)
 
@@ -178,7 +179,7 @@
             def _():
                 tell(ready_b, {"narrow": n - 1})
 
-        @pl.when(even & jnp.logical_not(owner))
+        @pl.when(even & (z != home_a))
         def _():
             pl.semaphore_wait(ready_a, 1)
 
@@ -386,19 +387,29 @@
     send2[...] = jnp.sum(recv1[...].astype(F32), axis=0).astype(BF16)
 
     deliver = pltpu.make_async_remote_copy(
-        send2, recv2.at[z], sem_send2, sem_recv2, device_id={"narrow": w}, device_id_type=MESH
-    )
-
-    @pl.when(jnp.logical_not(owner))
+        send2, recv2.at[z], sem_send2, sem_recv2, device_id={"wide": home_b, "narrow": w}, device_id_type=MESH
+    )
+
+    @pl.when(jnp.logical_not(own_b))
     def _():
         deliver.start()
         deliver.wait_send()
+
+    @pl.when(jnp.logical_not(owner))
+    def _():
         pltpu.make_async_copy(final, final, sem_recv3).wait()
 
-    @pl.when(owner)
+    @pl.when(own_a)
+    def _():
+        pltpu.make_async_copy(recv2, recv2, sem_recv2).wait()
+
+    @pl.when(own_b)
     def _():
         recv2[z] = send2[...]
         pltpu.make_async_copy(recv2.at[pl.ds(0, n - 1)], recv2.at[pl.ds(0, n - 1)], sem_recv2).wait()
+
+    @pl.when(owner)
+    def _():
         whole = jnp.sum(recv2[...].astype(F32), axis=0).astype(BF16)
         send3[...] = whole
         final[...] = whole

time: 50.6 us -> 49.9 us (0.986)
  no operation moved by 1% of the time
where the time goes in v6:
time: 49.9 us; the launch traced here: 49.8 us
  Pallas kernels  47.8 us (96%)
  local copies, waits for them, and re-layouts  1.31 us (3%)
  between operations  0.64 us (1%)
    pallas_call x1, Pallas kernels, body(): pl.pallas_call(functools.partial(kernel, n, scale), out_shape=(jax.ShapeD...  47.8 us
    unnamed x2, local copies, waits for them, and re-layouts  1.31 us

profile of v6, /device:TPU:1, one launch (start us, length us, event | category | flops | bytes accessed | tf_op | source)
XLA Modules:
  0.0 49.8 jit_solution(6305676854553461446)
XLA Ops:
  0.6 47.8 %shard_map.77 = (bf16[64,2048]{1,0:T(8,128)(2,1)S(1)}, f32[27,2,32]{2,1,0:T(2,128)S(1)}) custom-call(bf16[4,4,4096]{2,1,0:T(4,128)(2,1)} %bitcast.8, bf16[64,64]{1,0:T(8,128)(2,1)} %constant.4.clone.rows_hbm, bf16[256,128]{1,0:T(8,128)(2,1)} %constant.5.clone.places_hbm, bf16[27,4,32]{2,1,0:T(4,128)(2,1)} %bitcast.9, bf16[27,32,64]{2,1,0:T(8,128)(2,1)} %bitcast.7, ...), custom_call_target="tpu_custom_call" | custom-call | tf_op jit(solution)/shard_map/pallas_call | solution.py:447
  48.5 0.7 %copy.10 = bf16[1,1,64,2048]{3,2,1,0:T(8,128)(2,1)} copy(bf16[1,1,64,2048]{3,2,1,0:T(8,128)(2,1)S(1)} %bitcast.5) | data formatting | bytes 524288
  49.2 0.6 %copy.11 = f32[27,2,32]{2,1,0:T(2,128)} copy(f32[27,2,32]{2,1,0:T(2,128)S(1)} %get-tuple-element.9) | data formatting | bytes 13824

commit v7 on v6

--- a/solution.py
+++ b/solution.py
@@ -313,14 +313,22 @@
             preferred_element_type=F32,
         )
 
-    def second_sum(half):
+    def second_pre(half):
         pre = None
         for a in range(3):
             at = C2 * reached[half + a].index(a)
             part = parts2[half + a, at : at + C2, :]
             pre = part if pre is None else pre + part
+        return pre
+
+    def second_act(half):
+        pre = second_pre(half)
         cells = slice(PLANE * half, PLANE * half + PLANE)
         act_ref[:, cells] = jnp.where(pre > 0, pre, SLOPE * pre).astype(BF16)
+
+    def second_sum(half):
+        pre = second_pre(half)
+        cells = slice(PLANE * half, PLANE * half + PLANE)
         backs[half] = (cot_ref[:, cells].astype(F32) * jnp.where(pre > 0, 1.0, SLOPE)).astype(BF16)
 
     def gradient_part(zo):
@@ -381,6 +389,8 @@
             send1.at[to], recv1.at[w], sem_send1, sem_recv1, device_id={"wide": to}, device_id_type=MESH
         ).start()
     relay()
+    second_act(0)
+    second_act(1)
     pltpu.make_async_copy(send1.at[pl.ds(0, n - 1)], send1.at[pl.ds(0, n - 1)], sem_send1).wait()
     pltpu.make_async_copy(recv1.at[pl.ds(0, n - 1)], recv1.at[pl.ds(0, n - 1)], sem_recv1).wait()
 

time: 49.9 us -> 49.9 us (level)
  no operation moved by 1% of the time
where the time goes in v7:
time: 49.9 us; the launch traced here: 49.8 us
  Pallas kernels  47.8 us (96%)
  local copies, waits for them, and re-layouts  1.31 us (3%)
  between operations  0.64 us (1%)
    pallas_call x1, Pallas kernels, body(): pl.pallas_call(functools.partial(kernel, n, scale), out_shape=(jax.ShapeD...  47.8 us
    unnamed x2, local copies, waits for them, and re-layouts  1.31 us

profile of v7, /device:TPU:1, one launch (start us, length us, event | category | flops | bytes accessed | tf_op | source)
XLA Modules:
  0.0 49.8 jit_solution(2288684076053499845)
XLA Ops:
  0.6 47.8 %shard_map.77 = (bf16[64,2048]{1,0:T(8,128)(2,1)S(1)}, f32[27,2,32]{2,1,0:T(2,128)S(1)}) custom-call(bf16[4,4,4096]{2,1,0:T(4,128)(2,1)} %bitcast.8, bf16[64,64]{1,0:T(8,128)(2,1)} %constant.4.clone.rows_hbm, bf16[256,128]{1,0:T(8,128)(2,1)} %constant.5.clone.places_hbm, bf16[27,4,32]{2,1,0:T(4,128)(2,1)} %bitcast.9, bf16[27,32,64]{2,1,0:T(8,128)(2,1)} %bitcast.7, ...), custom_call_target="tpu_custom_call" | custom-call | tf_op jit(solution)/shard_map/pallas_call | solution.py:457
  48.4 0.7 %copy.10 = bf16[1,1,64,2048]{3,2,1,0:T(8,128)(2,1)} copy(bf16[1,1,64,2048]{3,2,1,0:T(8,128)(2,1)S(1)} %bitcast.5) | data formatting | bytes 524288
  49.2 0.6 %copy.11 = f32[27,2,32]{2,1,0:T(2,128)} copy(f32[27,2,32]{2,1,0:T(2,128)S(1)} %get-tuple-element.9) | data formatting | bytes 13824
